TPU v7x, 128 devices: a whole 4x4x4 slice. The times are simulated.
128 devices in a mesh: chan: 32 (over x, z_hi, y), grp: 4 (over z_lo, core).
Axes of the slice: x: 4, y: 4, z: 4 (z_hi: 2, z_lo: 2; z = z_hi * 2 + z_lo), core: 2. Of those that a mesh axis runs over, the one named last changes fastest.
Arguments:
- voltages: bfloat16 [512, 4096, 128], P(('chan', 'grp')), may hold values from -6 to 6
- delays: int32 [64, 512], replicated, may hold values from 0 to 4095
- shifts: int32 [256, 512], replicated, may hold values from 0 to 511
Outputs:
- dm_power: float32 [256, 512, 256], P('grp', 'chan')
All inputs are finite; a program needn't handle non-finite values.
Results may differ from a plain program's by a relative error of at most 0.011.
Values may be sent and summed in bfloat16 or wider, within the bound.
No kernel may reach another device: no remote copies, remote signals or barrier semaphores. Data moves between devices by JAX's collectives and lax.ppermute only.
A program may use at most 128 MiB of HBM per device.

v0:
```python
import math
import jax
import jax.numpy as jnp
from jax import lax
from jax.sharding import PartitionSpec as P

DISHES = 64
INTEG = 8
PHASES = 4096
KBLK = 16


def beam_matrix(delays, channel, channel_count):
    frequency = channel + channel_count
    residue = jnp.mod(delays * frequency, PHASES)
    phases = residue.astype(jnp.float32) * jnp.float32(2.0 * math.pi / PHASES)
    weight_scale = jnp.float32(1.0 / math.sqrt(DISHES))
    real_part = jnp.cos(phases) * weight_scale
    imag_part = -jnp.sin(phases) * weight_scale
    upper = jnp.concatenate([real_part, imag_part], axis=1)
    lower = jnp.concatenate([-imag_part, real_part], axis=1)
    return jnp.concatenate([upper, lower], axis=0).astype(jnp.bfloat16)


def detect(samples, matrix):
    beams = jnp.dot(samples, matrix, preferred_element_type=jnp.float32)
    half_width = matrix.shape[1] // 2
    intensity = beams[:, :half_width] ** 2 + beams[:, half_width:] ** 2
    steps_count = samples.shape[0] // INTEG
    averaged = jnp.sum(intensity.reshape(steps_count, INTEG, half_width), axis=1) * jnp.float32(
        1.0 / INTEG
    )
    return averaged.T.astype(jnp.bfloat16)


def dft_table(length):
    bins_count = length // 2
    sample_index = jnp.arange(length, dtype=jnp.int32)[:, None]
    freq_index = jnp.arange(1, bins_count + 1, dtype=jnp.int32)[None, :]
    residue = jnp.mod(sample_index * freq_index, length)
    phases = residue.astype(jnp.float32) * jnp.float32(2.0 * math.pi / length)
    norm_scale = jnp.float32(1.0 / math.sqrt(length))
    return jnp.concatenate(
        [jnp.cos(phases) * norm_scale, -jnp.sin(phases) * norm_scale], axis=1
    ).astype(jnp.bfloat16)


def spectra(series, table):
    flat = series.reshape(-1, series.shape[-1])
    result = jnp.dot(flat, table, preferred_element_type=jnp.float32).astype(jnp.bfloat16)
    return result.reshape(series.shape[:-1] + (table.shape[1],))


def dedisperse(spectrum, selected, phase_scale):
    channel_count, beam_count, doubled = spectrum.shape
    bins_count = doubled // 2
    trial_count = selected.shape[0]
    parted = spectrum.reshape(channel_count, beam_count, 2, bins_count).transpose(2, 3, 1, 0)
    real_spec = parted[0]
    imag_spec = parted[1]
    across = selected.T

    def one_block(block_index):
        start = block_index * KBLK
        real_piece = lax.dynamic_slice_in_dim(real_spec, start, KBLK, 0)
        imag_piece = lax.dynamic_slice_in_dim(imag_spec, start, KBLK, 0)
        freq_index = (start + jnp.arange(KBLK, dtype=jnp.int32) + 1)[:, None, None]
        residue = jnp.mod(freq_index * across[None, :, :], doubled)
        phases = residue.astype(jnp.float32) * jnp.float32(2.0 * math.pi / doubled)
        cosine = (jnp.cos(phases) * phase_scale).astype(jnp.bfloat16)
        sine = (jnp.sin(phases) * phase_scale).astype(jnp.bfloat16)
        cos_real = jnp.einsum(
            "kbc,kcm->kbm", real_piece, cosine, preferred_element_type=jnp.float32
        )
        sin_imag = jnp.einsum("kbc,kcm->kbm", imag_piece, sine, preferred_element_type=jnp.float32)
        sin_real = jnp.einsum("kbc,kcm->kbm", real_piece, sine, preferred_element_type=jnp.float32)
        cos_imag = jnp.einsum(
            "kbc,kcm->kbm", imag_piece, cosine, preferred_element_type=jnp.float32
        )
        return jnp.stack([cos_real - sin_imag, sin_real + cos_imag], axis=1)

    blocks = lax.map(one_block, jnp.arange(bins_count // KBLK, dtype=jnp.int32))
    return blocks.reshape(bins_count, 2, beam_count, trial_count)


def body(voltages, delays, shifts):
    chan_count = lax.axis_size("chan")
    group_count = lax.axis_size("grp")
    chan_local = voltages.shape[0]
    channel_total = chan_local * chan_count * group_count
    first_channel = (lax.axis_index("chan") * group_count + lax.axis_index("grp")) * chan_local

    def detect_channel(item):
        samples, offset = item
        return detect(samples, beam_matrix(delays, first_channel + offset, channel_total))

    detected = lax.map(detect_channel, (voltages, jnp.arange(chan_local, dtype=jnp.int32)))
    table = dft_table(detected.shape[2])
    phase_scale = jnp.float32(1.0 / math.sqrt(channel_total))
    trial_count = shifts.shape[0]
    grouped = shifts.reshape(trial_count, chan_count, group_count, chan_local)
    selected = lax.dynamic_index_in_dim(grouped, lax.axis_index("grp"), axis=2, keepdims=False)
    selected = selected.reshape(trial_count, chan_count * chan_local)
    beam_total = detected.shape[1]
    blocked = detected.reshape(chan_local, chan_count, beam_total // chan_count, detected.shape[2])
    partial_spec = dedisperse(
        spectra(
            lax.all_to_all(blocked, "chan", split_axis=1, concat_axis=0, tiled=True)[:, 0], table
        ),
        selected,
        phase_scale,
    )
    summed = lax.psum_scatter(partial_spec, "grp", scatter_dimension=3, tiled=True)
    result = summed[:, 0] ** 2 + summed[:, 1] ** 2
    return result.transpose(2, 1, 0)


def solution(mesh):
    placed = (P(("chan", "grp"), None, None), P(), P())
    return jax.shard_map(
        body, mesh=mesh, in_specs=placed, out_specs=P("grp", "chan", None), check_vma=False
    )
```

profile of v0, /device:TPU:1, one launch (start us, length us, event | category | flops | bytes accessed | tf_op | source)
XLA Modules:
  0.0 781.8 jit_solution(4878138713700647623)
XLA Ops:
  6.5 39.4 %while.24 = (s32[]{:T(128)}, bf16[4,512,512]{2,1,0:T(8,128)(2,1)S(1)}, bf16[4,4096,128]{2,1,0:T(8,128)(2,1)}, s32[4]{0:T(128)S(1)}, s32[]{:T(128)}, /*index=5*/s32[64,512]{1,0:T(8,128)}, s32[]{:T(128)}, s32[]{:T(128)}) while((s32[]{:T(128)}, bf16[4,512,512]{2,1,0:T(8,128)(2,1)S(1)}, bf16[4,4096,128]{2,1,0:T(8,128)(2,1)}, s32[4]{0:T(128)S(1)}, ...), condition=%wide.region_2.3_spmd, body=%wide.region_0.2_spmd.sunk | while | flops 1084129280 | bytes 39846528 | solution.py:97
  47.6 11.3 %all-to-all-start = ((bf16[4,32,16,512]{3,2,0,1:T(8,128)(2,1)}), bf16[4,32,16,512]{3,2,0,1:T(8,128)(2,1)S(1)}, u32[]{:S(2)}, u32[]{:S(2)}) async-start(bf16[4,32,16,512]{3,2,0,1:T(8,128)(2,1)} %copy.17), calls=%async_computation | async-start | bytes 4194304 | tf_op jit(solution)/shard_map/all_to_all | solution.py:108
  61.7 25.5 %all-to-all-done = bf16[4,32,16,512]{3,2,0,1:T(8,128)(2,1)S(1)} async-done(((bf16[4,32,16,512]{3,2,0,1:T(8,128)(2,1)}), bf16[4,32,16,512]{3,2,0,1:T(8,128)(2,1)S(1)}, u32[]{:S(2)}, u32[]{:S(2)}) %all-to-all-start) | async-done | bytes 2097184 | tf_op jit(solution)/shard_map/all_to_all | solution.py:108
  99.1 583.7 %while.25 = (s32[]{:T(128)}, f32[16,16,2,16,256]{4,3,2,1,0:T(8,128)}, s32[16]{0:T(128)S(1)}, bf16[256,16,128]{2,1,0:T(8,128)(2,1)}, s32[128,256]{1,0:T(8,128)S(1...) while((s32[]{:T(128)}, f32[16,16,2,16,256]{4,3,2,1,0:T(8,128)}, ...), condition=%wide.region_4.5_spmd, body=%wide.region_3.4_spmd.sunk | while | flops 100925472 | bytes 3409779 | solution.py:82
  122.3 8.6 %fusion.90 = f32[16,16,256]{2,1,0:T(8,128)S(1)} fusion(s32[128,256]{1,0:T(8,128)S(1)} %get-tuple-element.322, s32[16]{0:T(128)S(1)} %add_add_fusion.2, bf16[256,16,128]{2,1,0:T(8,128)(2,1)} %get-tuple-element.321, s32[]{:T(128)S(6)} %select_n.88), kind=kOutput, calls=%fused_computation.44.clone.1 | convolution fusion | flops 25165824 | bytes 458820 | tf_op jit(solution)/shard_map/while/body/eval_jaxpr/kbc,kcm->kbm/dot_general | solution.py:72
  138.8 8.7 %fusion.88 = f32[16,16,256]{2,1,0:T(8,128)S(1)} fusion(s32[128,256]{1,0:T(8,128)S(1)} %get-tuple-element.322, s32[16]{0:T(128)S(1)} %add_add_fusion.2, bf16[256,16,128]{2,1,0:T(8,128)(2,1)} %get-tuple-element.321, s32[]{:T(128)S(6)} %select_n.88), kind=kOutput, calls=%fused_computation.45.clone.1 | convolution fusion | flops 25165824 | bytes 458820 | tf_op jit(solution)/shard_map/while/body/eval_jaxpr/kbc,kcm->kbm/dot_general | solution.py:76
  157.4 8.6 %fusion.90 = f32[16,16,256]{2,1,0:T(8,128)S(1)} fusion(s32[128,256]{1,0:T(8,128)S(1)} %get-tuple-element.322, s32[16]{0:T(128)S(1)} %add_add_fusion.2, bf16[256,16,128]{2,1,0:T(8,128)(2,1)} %get-tuple-element.321, s32[]{:T(128)S(6)} %select_n.88), kind=kOutput, calls=%fused_computation.44.clone.1 | convolution fusion | flops 25165824 | bytes 458820 | tf_op jit(solution)/shard_map/while/body/eval_jaxpr/kbc,kcm->kbm/dot_general | solution.py:72
  173.9 8.7 %fusion.88 = f32[16,16,256]{2,1,0:T(8,128)S(1)} fusion(s32[128,256]{1,0:T(8,128)S(1)} %get-tuple-element.322, s32[16]{0:T(128)S(1)} %add_add_fusion.2, bf16[256,16,128]{2,1,0:T(8,128)(2,1)} %get-tuple-element.321, s32[]{:T(128)S(6)} %select_n.88), kind=kOutput, calls=%fused_computation.45.clone.1 | convolution fusion | flops 25165824 | bytes 458820 | tf_op jit(solution)/shard_map/while/body/eval_jaxpr/kbc,kcm->kbm/dot_general | solution.py:76
  192.5 8.6 %fusion.90 = f32[16,16,256]{2,1,0:T(8,128)S(1)} fusion(s32[128,256]{1,0:T(8,128)S(1)} %get-tuple-element.322, s32[16]{0:T(128)S(1)} %add_add_fusion.2, bf16[256,16,128]{2,1,0:T(8,128)(2,1)} %get-tuple-element.321, s32[]{:T(128)S(6)} %select_n.88), kind=kOutput, calls=%fused_computation.44.clone.1 | convolution fusion | flops 25165824 | bytes 458820 | tf_op jit(solution)/shard_map/while/body/eval_jaxpr/kbc,kcm->kbm/dot_general | solution.py:72
  209.0 8.7 %fusion.88 = f32[16,16,256]{2,1,0:T(8,128)S(1)} fusion(s32[128,256]{1,0:T(8,128)S(1)} %get-tuple-element.322, s32[16]{0:T(128)S(1)} %add_add_fusion.2, bf16[256,16,128]{2,1,0:T(8,128)(2,1)} %get-tuple-element.321, s32[]{:T(128)S(6)} %select_n.88), kind=kOutput, calls=%fused_computation.45.clone.1 | convolution fusion | flops 25165824 | bytes 458820 | tf_op jit(solution)/shard_map/while/body/eval_jaxpr/kbc,kcm->kbm/dot_general | solution.py:76
  227.6 8.6 %fusion.90 = f32[16,16,256]{2,1,0:T(8,128)S(1)} fusion(s32[128,256]{1,0:T(8,128)S(1)} %get-tuple-element.322, s32[16]{0:T(128)S(1)} %add_add_fusion.2, bf16[256,16,128]{2,1,0:T(8,128)(2,1)} %get-tuple-element.321, s32[]{:T(128)S(6)} %select_n.88), kind=kOutput, calls=%fused_computation.44.clone.1 | convolution fusion | flops 25165824 | bytes 458820 | tf_op jit(solution)/shard_map/while/body/eval_jaxpr/kbc,kcm->kbm/dot_general | solution.py:72
  244.1 8.7 %fusion.88 = f32[16,16,256]{2,1,0:T(8,128)S(1)} fusion(s32[128,256]{1,0:T(8,128)S(1)} %get-tuple-element.322, s32[16]{0:T(128)S(1)} %add_add_fusion.2, bf16[256,16,128]{2,1,0:T(8,128)(2,1)} %get-tuple-element.321, s32[]{:T(128)S(6)} %select_n.88), kind=kOutput, calls=%fused_computation.45.clone.1 | convolution fusion | flops 25165824 | bytes 458820 | tf_op jit(solution)/shard_map/while/body/eval_jaxpr/kbc,kcm->kbm/dot_general | solution.py:76
  262.7 8.6 %fusion.90 = f32[16,16,256]{2,1,0:T(8,128)S(1)} fusion(s32[128,256]{1,0:T(8,128)S(1)} %get-tuple-element.322, s32[16]{0:T(128)S(1)} %add_add_fusion.2, bf16[256,16,128]{2,1,0:T(8,128)(2,1)} %get-tuple-element.321, s32[]{:T(128)S(6)} %select_n.88), kind=kOutput, calls=%fused_computation.44.clone.1 | convolution fusion | flops 25165824 | bytes 458820 | tf_op jit(solution)/shard_map/while/body/eval_jaxpr/kbc,kcm->kbm/dot_general | solution.py:72
  279.2 8.7 %fusion.88 = f32[16,16,256]{2,1,0:T(8,128)S(1)} fusion(s32[128,256]{1,0:T(8,128)S(1)} %get-tuple-element.322, s32[16]{0:T(128)S(1)} %add_add_fusion.2, bf16[256,16,128]{2,1,0:T(8,128)(2,1)} %get-tuple-element.321, s32[]{:T(128)S(6)} %select_n.88), kind=kOutput, calls=%fused_computation.45.clone.1 | convolution fusion | flops 25165824 | bytes 458820 | tf_op jit(solution)/shard_map/while/body/eval_jaxpr/kbc,kcm->kbm/dot_general | solution.py:76
  297.8 8.6 %fusion.90 = f32[16,16,256]{2,1,0:T(8,128)S(1)} fusion(s32[128,256]{1,0:T(8,128)S(1)} %get-tuple-element.322, s32[16]{0:T(128)S(1)} %add_add_fusion.2, bf16[256,16,128]{2,1,0:T(8,128)(2,1)} %get-tuple-element.321, s32[]{:T(128)S(6)} %select_n.88), kind=kOutput, calls=%fused_computation.44.clone.1 | convolution fusion | flops 25165824 | bytes 458820 | tf_op jit(solution)/shard_map/while/body/eval_jaxpr/kbc,kcm->kbm/dot_general | solution.py:72
  314.3 8.7 %fusion.88 = f32[16,16,256]{2,1,0:T(8,128)S(1)} fusion(s32[128,256]{1,0:T(8,128)S(1)} %get-tuple-element.322, s32[16]{0:T(128)S(1)} %add_add_fusion.2, bf16[256,16,128]{2,1,0:T(8,128)(2,1)} %get-tuple-element.321, s32[]{:T(128)S(6)} %select_n.88), kind=kOutput, calls=%fused_computation.45.clone.1 | convolution fusion | flops 25165824 | bytes 458820 | tf_op jit(solution)/shard_map/while/body/eval_jaxpr/kbc,kcm->kbm/dot_general | solution.py:76
  349.4 8.7 %fusion.88 = f32[16,16,256]{2,1,0:T(8,128)S(1)} fusion(s32[128,256]{1,0:T(8,128)S(1)} %get-tuple-element.322, s32[16]{0:T(128)S(1)} %add_add_fusion.2, bf16[256,16,128]{2,1,0:T(8,128)(2,1)} %get-tuple-element.321, s32[]{:T(128)S(6)} %select_n.88), kind=kOutput, calls=%fused_computation.45.clone.1 | convolution fusion | flops 25165824 | bytes 458820 | tf_op jit(solution)/shard_map/while/body/eval_jaxpr/kbc,kcm->kbm/dot_general | solution.py:76
  368.0 8.6 %fusion.90 = f32[16,16,256]{2,1,0:T(8,128)S(1)} fusion(s32[128,256]{1,0:T(8,128)S(1)} %get-tuple-element.322, s32[16]{0:T(128)S(1)} %add_add_fusion.2, bf16[256,16,128]{2,1,0:T(8,128)(2,1)} %get-tuple-element.321, s32[]{:T(128)S(6)} %select_n.88), kind=kOutput, calls=%fused_computation.44.clone.1 | convolution fusion | flops 25165824 | bytes 458820 | tf_op jit(solution)/shard_map/while/body/eval_jaxpr/kbc,kcm->kbm/dot_general | solution.py:72
  384.5 8.7 %fusion.88 = f32[16,16,256]{2,1,0:T(8,128)S(1)} fusion(s32[128,256]{1,0:T(8,128)S(1)} %get-tuple-element.322, s32[16]{0:T(128)S(1)} %add_add_fusion.2, bf16[256,16,128]{2,1,0:T(8,128)(2,1)} %get-tuple-element.321, s32[]{:T(128)S(6)} %select_n.88), kind=kOutput, calls=%fused_computation.45.clone.1 | convolution fusion | flops 25165824 | bytes 458820 | tf_op jit(solution)/shard_map/while/body/eval_jaxpr/kbc,kcm->kbm/dot_general | solution.py:76
  403.1 8.6 %fusion.90 = f32[16,16,256]{2,1,0:T(8,128)S(1)} fusion(s32[128,256]{1,0:T(8,128)S(1)} %get-tuple-element.322, s32[16]{0:T(128)S(1)} %add_add_fusion.2, bf16[256,16,128]{2,1,0:T(8,128)(2,1)} %get-tuple-element.321, s32[]{:T(128)S(6)} %select_n.88), kind=kOutput, calls=%fused_computation.44.clone.1 | convolution fusion | flops 25165824 | bytes 458820 | tf_op jit(solution)/shard_map/while/body/eval_jaxpr/kbc,kcm->kbm/dot_general | solution.py:72
  419.6 8.7 %fusion.88 = f32[16,16,256]{2,1,0:T(8,128)S(1)} fusion(s32[128,256]{1,0:T(8,128)S(1)} %get-tuple-element.322, s32[16]{0:T(128)S(1)} %add_add_fusion.2, bf16[256,16,128]{2,1,0:T(8,128)(2,1)} %get-tuple-element.321, s32[]{:T(128)S(6)} %select_n.88), kind=kOutput, calls=%fused_computation.45.clone.1 | convolution fusion | flops 25165824 | bytes 458820 | tf_op jit(solution)/shard_map/while/body/eval_jaxpr/kbc,kcm->kbm/dot_general | solution.py:76
  454.7 8.7 %fusion.88 = f32[16,16,256]{2,1,0:T(8,128)S(1)} fusion(s32[128,256]{1,0:T(8,128)S(1)} %get-tuple-element.322, s32[16]{0:T(128)S(1)} %add_add_fusion.2, bf16[256,16,128]{2,1,0:T(8,128)(2,1)} %get-tuple-element.321, s32[]{:T(128)S(6)} %select_n.88), kind=kOutput, calls=%fused_computation.45.clone.1 | convolution fusion | flops 25165824 | bytes 458820 | tf_op jit(solution)/shard_map/while/body/eval_jaxpr/kbc,kcm->kbm/dot_general | solution.py:76
  489.8 8.7 %fusion.88 = f32[16,16,256]{2,1,0:T(8,128)S(1)} fusion(s32[128,256]{1,0:T(8,128)S(1)} %get-tuple-element.322, s32[16]{0:T(128)S(1)} %add_add_fusion.2, bf16[256,16,128]{2,1,0:T(8,128)(2,1)} %get-tuple-element.321, s32[]{:T(128)S(6)} %select_n.88), kind=kOutput, calls=%fused_computation.45.clone.1 | convolution fusion | flops 25165824 | bytes 458820 | tf_op jit(solution)/shard_map/while/body/eval_jaxpr/kbc,kcm->kbm/dot_general | solution.py:76
  525.0 8.7 %fusion.88 = f32[16,16,256]{2,1,0:T(8,128)S(1)} fusion(s32[128,256]{1,0:T(8,128)S(1)} %get-tuple-element.322, s32[16]{0:T(128)S(1)} %add_add_fusion.2, bf16[256,16,128]{2,1,0:T(8,128)(2,1)} %get-tuple-element.321, s32[]{:T(128)S(6)} %select_n.88), kind=kOutput, calls=%fused_computation.45.clone.1 | convolution fusion | flops 25165824 | bytes 458820 | tf_op jit(solution)/shard_map/while/body/eval_jaxpr/kbc,kcm->kbm/dot_general | solution.py:76
  560.1 8.7 %fusion.88 = f32[16,16,256]{2,1,0:T(8,128)S(1)} fusion(s32[128,256]{1,0:T(8,128)S(1)} %get-tuple-element.322, s32[16]{0:T(128)S(1)} %add_add_fusion.2, bf16[256,16,128]{2,1,0:T(8,128)(2,1)} %get-tuple-element.321, s32[]{:T(128)S(6)} %select_n.88), kind=kOutput, calls=%fused_computation.45.clone.1 | convolution fusion | flops 25165824 | bytes 458820 | tf_op jit(solution)/shard_map/while/body/eval_jaxpr/kbc,kcm->kbm/dot_general | solution.py:76
  578.7 8.6 %fusion.90 = f32[16,16,256]{2,1,0:T(8,128)S(1)} fusion(s32[128,256]{1,0:T(8,128)S(1)} %get-tuple-element.322, s32[16]{0:T(128)S(1)} %add_add_fusion.2, bf16[256,16,128]{2,1,0:T(8,128)(2,1)} %get-tuple-element.321, s32[]{:T(128)S(6)} %select_n.88), kind=kOutput, calls=%fused_computation.44.clone.1 | convolution fusion | flops 25165824 | bytes 458820 | tf_op jit(solution)/shard_map/while/body/eval_jaxpr/kbc,kcm->kbm/dot_general | solution.py:72
  595.2 8.7 %fusion.88 = f32[16,16,256]{2,1,0:T(8,128)S(1)} fusion(s32[128,256]{1,0:T(8,128)S(1)} %get-tuple-element.322, s32[16]{0:T(128)S(1)} %add_add_fusion.2, bf16[256,16,128]{2,1,0:T(8,128)(2,1)} %get-tuple-element.321, s32[]{:T(128)S(6)} %select_n.88), kind=kOutput, calls=%fused_computation.45.clone.1 | convolution fusion | flops 25165824 | bytes 458820 | tf_op jit(solution)/shard_map/while/body/eval_jaxpr/kbc,kcm->kbm/dot_general | solution.py:76
  613.8 8.6 %fusion.90 = f32[16,16,256]{2,1,0:T(8,128)S(1)} fusion(s32[128,256]{1,0:T(8,128)S(1)} %get-tuple-element.322, s32[16]{0:T(128)S(1)} %add_add_fusion.2, bf16[256,16,128]{2,1,0:T(8,128)(2,1)} %get-tuple-element.321, s32[]{:T(128)S(6)} %select_n.88), kind=kOutput, calls=%fused_computation.44.clone.1 | convolution fusion | flops 25165824 | bytes 458820 | tf_op jit(solution)/shard_map/while/body/eval_jaxpr/kbc,kcm->kbm/dot_general | solution.py:72
  630.3 8.7 %fusion.88 = f32[16,16,256]{2,1,0:T(8,128)S(1)} fusion(s32[128,256]{1,0:T(8,128)S(1)} %get-tuple-element.322, s32[16]{0:T(128)S(1)} %add_add_fusion.2, bf16[256,16,128]{2,1,0:T(8,128)(2,1)} %get-tuple-element.321, s32[]{:T(128)S(6)} %select_n.88), kind=kOutput, calls=%fused_computation.45.clone.1 | convolution fusion | flops 25165824 | bytes 458820 | tf_op jit(solution)/shard_map/while/body/eval_jaxpr/kbc,kcm->kbm/dot_general | solution.py:76
  665.4 8.7 %fusion.88 = f32[16,16,256]{2,1,0:T(8,128)S(1)} fusion(s32[128,256]{1,0:T(8,128)S(1)} %get-tuple-element.322, s32[16]{0:T(128)S(1)} %add_add_fusion.2, bf16[256,16,128]{2,1,0:T(8,128)(2,1)} %get-tuple-element.321, s32[]{:T(128)S(6)} %select_n.88), kind=kOutput, calls=%fused_computation.45.clone.1 | convolution fusion | flops 25165824 | bytes 458820 | tf_op jit(solution)/shard_map/while/body/eval_jaxpr/kbc,kcm->kbm/dot_general | solution.py:76
  682.8 10.5 %copy.21 = f32[256,2,16,256]{0,2,1,3:T(8,128)} copy(f32[256,2,16,256]{3,2,1,0:T(8,128)} %bitcast.17) | data formatting | bytes 16777216 | tf_op jit(solution)/shard_map/reshape | solution.py:83
  693.3 78.6 %reduce-scatter.2.cloned.1.call-done = f32[256,2,16,64]{0,2,1,3:T(8,128)} async-done(((f32[256,2,16,256]{0,2,1,3:T(8,128)}), f32[256,2,16,64]{0,2,1,3:T(8,128)}) %reduce-scatter.2.cloned.1.call-update) | async-done | bytes 2097168 | tf_op jit(solution)/shard_map/reduce_scatter | solution.py:113
  (134 shorter events, 381.6 us)
Async XLA Ops:
  47.6 11.4 %copy-start = (s32[256,512]{1,0:T(8,128)S(1)}, s32[256,512]{1,0:T(8,128)}, u32[]{:S(2)}) copy-start(s32[256,512]{1,0:T(8,128)} %param.9) | copy-start | bytes 1572868
  47.6 39.6 %all-to-all-start = ((bf16[4,32,16,512]{3,2,0,1:T(8,128)(2,1)}), bf16[4,32,16,512]{3,2,0,1:T(8,128)(2,1)S(1)}, u32[]{:S(2)}, u32[]{:S(2)}) async-start(bf16[4,32,16,512]{3,2,0,1:T(8,128)(2,1)} %copy.17), calls=%async_computation | async-start | bytes 4194304 | tf_op jit(solution)/shard_map/all_to_all | solution.py:108
  58.9 712.9 %reduce-scatter.2.cloned.1.call-start = ((), (), s32[]{:S(2)}) async-start(), calls=%async_computation.2 | async-start | bytes 10485760 | tf_op jit(solution)/shard_map/reduce_scatter | solution.py:113
Sparse Core Ops, SparseCore 0:
  693.4 78.4 reduce-scatter.1
where the time goes:
time: 791 us; the launch traced here: 782 us
  matrix products  545 us (69%)
  waiting for transfers between devices  104 us (13%)
  other arithmetic  37.2 us (5%)
  local copies, waits for them, and re-layouts  35.7 us (5%)
  loops' own time  35.1 us (4%)
  between operations  13.9 us (2%)
  starting transfers between devices  11.4 us (1%)
    dot_general x16, matrix products, one_block(): jnp.einsum('kbc,kcm->kbm', real_piece, sine, preferred_element_type=jnp.f...  139 us
    dot_general x16, matrix products, one_block(): jnp.einsum('kbc,kcm->kbm', real_piece, cosine, preferred_element_type=jnp...  138 us
    dot_general x16, matrix products, one_block(): jnp.einsum('kbc,kcm->kbm', imag_piece, sine, preferred_element_type=jnp.f...  126 us
    dot_general x16, matrix products, one_block(): jnp.einsum('kbc,kcm->kbm', imag_piece, cosine, preferred_element_type=jnp...  125 us
    reduce_scatter x1, waiting for transfers between devices, body(): lax.psum_scatter(partial_spec, 'grp', scatter_dimension=3, tiled=True)  78.6 us
    another operation x1, loops' own time, dedisperse(): blocks = lax.map(one_block, jnp.arange(bins_count // KBLK, dtype=jnp.int32))  32.2 us
    all_to_all x1, waiting for transfers between devices, body(): lax.all_to_all(blocked, 'chan', split_axis=1, concat_axis=0, tiled=True)  25.5 us
  transfers between devices with their start and end apart: 2, of which 2 were waited for; matrix products, arithmetic and copies ran while one was open for 0% of the time, Pallas kernels for 0%

commit v1 on v0

--- a/solution.py
+++ b/solution.py
@@ -105,7 +105,13 @@
     blocked = detected.reshape(chan_local, chan_count, beam_total // chan_count, detected.shape[2])
     partial_spec = dedisperse(
         spectra(
-            lax.all_to_all(blocked, "chan", split_axis=1, concat_axis=0, tiled=True)[:, 0], table
+            jnp.concatenate(
+                lax.all_to_all(
+                    jnp.stack(jnp.split(blocked, lax.axis_size("chan"), axis=1)), "chan", 0, 0
+                ),
+                axis=0,
+            )[:, 0],
+            table,
         ),
         selected,
         phase_scale,

time: 791 us -> 809 us (1.023)
  local copies, waits for them, and re-layouts: 35.7 us -> 54.1 us
    unnamed x3 -> x34, local copies, waits for them, and re-layouts: 0.2 us -> 19.5 us
where the time goes in v1:
time: 809 us; the launch traced here: 800 us
  matrix products  545 us (67%)
  waiting for transfers between devices  104 us (13%)
  local copies, waits for them, and re-layouts  54.1 us (7%)
  other arithmetic  37.2 us (5%)
  loops' own time  35.1 us (4%)
  between operations  13.9 us (2%)
  starting transfers between devices  11.4 us (1%)
    dot_general x16, matrix products, one_block(): jnp.einsum('kbc,kcm->kbm', real_piece, sine, preferred_element_type=jnp.f...  139 us
    dot_general x16, matrix products, one_block(): jnp.einsum('kbc,kcm->kbm', real_piece, cosine, preferred_element_type=jnp...  138 us
    dot_general x16, matrix products, one_block(): jnp.einsum('kbc,kcm->kbm', imag_piece, sine, preferred_element_type=jnp.f...  126 us
    dot_general x16, matrix products, one_block(): jnp.einsum('kbc,kcm->kbm', imag_piece, cosine, preferred_element_type=jnp...  125 us
    reduce_scatter x1, waiting for transfers between devices, body(): lax.psum_scatter(partial_spec, 'grp', scatter_dimension=3, tiled=True)  78.6 us
    another operation x1, loops' own time, dedisperse(): blocks = lax.map(one_block, jnp.arange(bins_count // KBLK, dtype=jnp.int32))  32.2 us
    all_to_all x1, waiting for transfers between devices, body(): lax.all_to_all(jnp.stack(jnp.split(blocked, lax.axis_size('chan'), axis=1...  25.5 us
    unnamed x34, local copies, waits for them, and re-layouts  19.5 us
  transfers between devices with their start and end apart: 2, of which 2 were waited for; matrix products, arithmetic and copies ran while one was open for 0% of the time, Pallas kernels for 0%

profile of v1, /device:TPU:1, one launch (start us, length us, event | category | flops | bytes accessed | tf_op | source)
XLA Modules:
  0.0 800.2 jit_solution(8520197458898960704)
XLA Ops:
  6.5 39.4 %while.24 = (s32[]{:T(128)}, bf16[4,512,512]{2,1,0:T(8,128)(2,1)S(1)}, bf16[4,4096,128]{2,1,0:T(8,128)(2,1)}, s32[4]{0:T(128)S(1)}, s32[]{:T(128)}, /*index=5*/s32[64,512]{1,0:T(8,128)}, s32[]{:T(128)}, s32[]{:T(128)}) while((s32[]{:T(128)}, bf16[4,512,512]{2,1,0:T(8,128)(2,1)S(1)}, bf16[4,4096,128]{2,1,0:T(8,128)(2,1)}, s32[4]{0:T(128)S(1)}, ...), condition=%wide.region_2.3_spmd, body=%wide.region_0.2_spmd.sunk | while | flops 1084129280 | bytes 39846528 | solution.py:97
  66.0 11.3 %all-to-all-start = ((bf16[32,4,1,16,512]{4,3,1,2,0:T(8,128)(2,1)}), bf16[32,4,1,16,512]{4,3,1,2,0:T(8,128)(2,1)S(1)}, u32[]{:S(2)}, u32[]{:S(2)}) async-start(bf16[32,4,1,16,512]{4,3,1,2,0:T(8,128)(2,1)} %constant_dynamic-update-slice_fusion.1), calls=%async_computation | async-start | bytes 4194304 | tf_op jit(solution)/shard_map/all_to_all | solution.py:109
  80.1 25.5 %all-to-all-done = bf16[32,4,1,16,512]{4,3,1,2,0:T(8,128)(2,1)S(1)} async-done(((bf16[32,4,1,16,512]{4,3,1,2,0:T(8,128)(2,1)}), bf16[32,4,1,16,512]{4,3,1,2,0:T(8,128)(2,1)S(1)}, u32[]{:S(2)}, u32[]{:S(2)}) %all-to-all-start) | async-done | bytes 2097184 | tf_op jit(solution)/shard_map/all_to_all | solution.py:109
  117.5 583.7 %while.25 = (s32[]{:T(128)}, f32[16,16,2,16,256]{4,3,2,1,0:T(8,128)}, s32[16]{0:T(128)S(1)}, bf16[256,16,128]{2,1,0:T(8,128)(2,1)}, s32[128,256]{1,0:T(8,128)S(1...) while((s32[]{:T(128)}, f32[16,16,2,16,256]{4,3,2,1,0:T(8,128)}, ...), condition=%wide.region_4.5_spmd, body=%wide.region_3.4_spmd.sunk | while | flops 100925472 | bytes 3409779 | solution.py:82
  140.6 8.6 %fusion.90 = f32[16,16,256]{2,1,0:T(8,128)S(1)} fusion(s32[128,256]{1,0:T(8,128)S(1)} %get-tuple-element.322, s32[16]{0:T(128)S(1)} %add_add_fusion.2, bf16[256,16,128]{2,1,0:T(8,128)(2,1)} %get-tuple-element.321, s32[]{:T(128)S(6)} %select_n.88), kind=kOutput, calls=%fused_computation.44.clone.1 | convolution fusion | flops 25165824 | bytes 458820 | tf_op jit(solution)/shard_map/while/body/eval_jaxpr/kbc,kcm->kbm/dot_general | solution.py:72
  157.1 8.7 %fusion.88 = f32[16,16,256]{2,1,0:T(8,128)S(1)} fusion(s32[128,256]{1,0:T(8,128)S(1)} %get-tuple-element.322, s32[16]{0:T(128)S(1)} %add_add_fusion.2, bf16[256,16,128]{2,1,0:T(8,128)(2,1)} %get-tuple-element.321, s32[]{:T(128)S(6)} %select_n.88), kind=kOutput, calls=%fused_computation.45.clone.1 | convolution fusion | flops 25165824 | bytes 458820 | tf_op jit(solution)/shard_map/while/body/eval_jaxpr/kbc,kcm->kbm/dot_general | solution.py:76
  175.7 8.6 %fusion.90 = f32[16,16,256]{2,1,0:T(8,128)S(1)} fusion(s32[128,256]{1,0:T(8,128)S(1)} %get-tuple-element.322, s32[16]{0:T(128)S(1)} %add_add_fusion.2, bf16[256,16,128]{2,1,0:T(8,128)(2,1)} %get-tuple-element.321, s32[]{:T(128)S(6)} %select_n.88), kind=kOutput, calls=%fused_computation.44.clone.1 | convolution fusion | flops 25165824 | bytes 458820 | tf_op jit(solution)/shard_map/while/body/eval_jaxpr/kbc,kcm->kbm/dot_general | solution.py:72
  192.2 8.7 %fusion.88 = f32[16,16,256]{2,1,0:T(8,128)S(1)} fusion(s32[128,256]{1,0:T(8,128)S(1)} %get-tuple-element.322, s32[16]{0:T(128)S(1)} %add_add_fusion.2, bf16[256,16,128]{2,1,0:T(8,128)(2,1)} %get-tuple-element.321, s32[]{:T(128)S(6)} %select_n.88), kind=kOutput, calls=%fused_computation.45.clone.1 | convolution fusion | flops 25165824 | bytes 458820 | tf_op jit(solution)/shard_map/while/body/eval_jaxpr/kbc,kcm->kbm/dot_general | solution.py:76
  210.8 8.6 %fusion.90 = f32[16,16,256]{2,1,0:T(8,128)S(1)} fusion(s32[128,256]{1,0:T(8,128)S(1)} %get-tuple-element.322, s32[16]{0:T(128)S(1)} %add_add_fusion.2, bf16[256,16,128]{2,1,0:T(8,128)(2,1)} %get-tuple-element.321, s32[]{:T(128)S(6)} %select_n.88), kind=kOutput, calls=%fused_computation.44.clone.1 | convolution fusion | flops 25165824 | bytes 458820 | tf_op jit(solution)/shard_map/while/body/eval_jaxpr/kbc,kcm->kbm/dot_general | solution.py:72
  227.3 8.7 %fusion.88 = f32[16,16,256]{2,1,0:T(8,128)S(1)} fusion(s32[128,256]{1,0:T(8,128)S(1)} %get-tuple-element.322, s32[16]{0:T(128)S(1)} %add_add_fusion.2, bf16[256,16,128]{2,1,0:T(8,128)(2,1)} %get-tuple-element.321, s32[]{:T(128)S(6)} %select_n.88), kind=kOutput, calls=%fused_computation.45.clone.1 | convolution fusion | flops 25165824 | bytes 458820 | tf_op jit(solution)/shard_map/while/body/eval_jaxpr/kbc,kcm->kbm/dot_general | solution.py:76
  246.0 8.6 %fusion.90 = f32[16,16,256]{2,1,0:T(8,128)S(1)} fusion(s32[128,256]{1,0:T(8,128)S(1)} %get-tuple-element.322, s32[16]{0:T(128)S(1)} %add_add_fusion.2, bf16[256,16,128]{2,1,0:T(8,128)(2,1)} %get-tuple-element.321, s32[]{:T(128)S(6)} %select_n.88), kind=kOutput, calls=%fused_computation.44.clone.1 | convolution fusion | flops 25165824 | bytes 458820 | tf_op jit(solution)/shard_map/while/body/eval_jaxpr/kbc,kcm->kbm/dot_general | solution.py:72
  262.5 8.7 %fusion.88 = f32[16,16,256]{2,1,0:T(8,128)S(1)} fusion(s32[128,256]{1,0:T(8,128)S(1)} %get-tuple-element.322, s32[16]{0:T(128)S(1)} %add_add_fusion.2, bf16[256,16,128]{2,1,0:T(8,128)(2,1)} %get-tuple-element.321, s32[]{:T(128)S(6)} %select_n.88), kind=kOutput, calls=%fused_computation.45.clone.1 | convolution fusion | flops 25165824 | bytes 458820 | tf_op jit(solution)/shard_map/while/body/eval_jaxpr/kbc,kcm->kbm/dot_general | solution.py:76
  281.1 8.6 %fusion.90 = f32[16,16,256]{2,1,0:T(8,128)S(1)} fusion(s32[128,256]{1,0:T(8,128)S(1)} %get-tuple-element.322, s32[16]{0:T(128)S(1)} %add_add_fusion.2, bf16[256,16,128]{2,1,0:T(8,128)(2,1)} %get-tuple-element.321, s32[]{:T(128)S(6)} %select_n.88), kind=kOutput, calls=%fused_computation.44.clone.1 | convolution fusion | flops 25165824 | bytes 458820 | tf_op jit(solution)/shard_map/while/body/eval_jaxpr/kbc,kcm->kbm/dot_general | solution.py:72
  297.6 8.7 %fusion.88 = f32[16,16,256]{2,1,0:T(8,128)S(1)} fusion(s32[128,256]{1,0:T(8,128)S(1)} %get-tuple-element.322, s32[16]{0:T(128)S(1)} %add_add_fusion.2, bf16[256,16,128]{2,1,0:T(8,128)(2,1)} %get-tuple-element.321, s32[]{:T(128)S(6)} %select_n.88), kind=kOutput, calls=%fused_computation.45.clone.1 | convolution fusion | flops 25165824 | bytes 458820 | tf_op jit(solution)/shard_map/while/body/eval_jaxpr/kbc,kcm->kbm/dot_general | solution.py:76
  316.2 8.6 %fusion.90 = f32[16,16,256]{2,1,0:T(8,128)S(1)} fusion(s32[128,256]{1,0:T(8,128)S(1)} %get-tuple-element.322, s32[16]{0:T(128)S(1)} %add_add_fusion.2, bf16[256,16,128]{2,1,0:T(8,128)(2,1)} %get-tuple-element.321, s32[]{:T(128)S(6)} %select_n.88), kind=kOutput, calls=%fused_computation.44.clone.1 | convolution fusion | flops 25165824 | bytes 458820 | tf_op jit(solution)/shard_map/while/body/eval_jaxpr/kbc,kcm->kbm/dot_general | solution.py:72
  332.7 8.7 %fusion.88 = f32[16,16,256]{2,1,0:T(8,128)S(1)} fusion(s32[128,256]{1,0:T(8,128)S(1)} %get-tuple-element.322, s32[16]{0:T(128)S(1)} %add_add_fusion.2, bf16[256,16,128]{2,1,0:T(8,128)(2,1)} %get-tuple-element.321, s32[]{:T(128)S(6)} %select_n.88), kind=kOutput, calls=%fused_computation.45.clone.1 | convolution fusion | flops 25165824 | bytes 458820 | tf_op jit(solution)/shard_map/while/body/eval_jaxpr/kbc,kcm->kbm/dot_general | solution.py:76
  351.3 8.6 %fusion.90 = f32[16,16,256]{2,1,0:T(8,128)S(1)} fusion(s32[128,256]{1,0:T(8,128)S(1)} %get-tuple-element.322, s32[16]{0:T(128)S(1)} %add_add_fusion.2, bf16[256,16,128]{2,1,0:T(8,128)(2,1)} %get-tuple-element.321, s32[]{:T(128)S(6)} %select_n.88), kind=kOutput, calls=%fused_computation.44.clone.1 | convolution fusion | flops 25165824 | bytes 458820 | tf_op jit(solution)/shard_map/while/body/eval_jaxpr/kbc,kcm->kbm/dot_general | solution.py:72
  367.8 8.7 %fusion.88 = f32[16,16,256]{2,1,0:T(8,128)S(1)} fusion(s32[128,256]{1,0:T(8,128)S(1)} %get-tuple-element.322, s32[16]{0:T(128)S(1)} %add_add_fusion.2, bf16[256,16,128]{2,1,0:T(8,128)(2,1)} %get-tuple-element.321, s32[]{:T(128)S(6)} %select_n.88), kind=kOutput, calls=%fused_computation.45.clone.1 | convolution fusion | flops 25165824 | bytes 458820 | tf_op jit(solution)/shard_map/while/body/eval_jaxpr/kbc,kcm->kbm/dot_general | solution.py:76
  386.4 8.6 %fusion.90 = f32[16,16,256]{2,1,0:T(8,128)S(1)} fusion(s32[128,256]{1,0:T(8,128)S(1)} %get-tuple-element.322, s32[16]{0:T(128)S(1)} %add_add_fusion.2, bf16[256,16,128]{2,1,0:T(8,128)(2,1)} %get-tuple-element.321, s32[]{:T(128)S(6)} %select_n.88), kind=kOutput, calls=%fused_computation.44.clone.1 | convolution fusion | flops 25165824 | bytes 458820 | tf_op jit(solution)/shard_map/while/body/eval_jaxpr/kbc,kcm->kbm/dot_general | solution.py:72
  402.9 8.7 %fusion.88 = f32[16,16,256]{2,1,0:T(8,128)S(1)} fusion(s32[128,256]{1,0:T(8,128)S(1)} %get-tuple-element.322, s32[16]{0:T(128)S(1)} %add_add_fusion.2, bf16[256,16,128]{2,1,0:T(8,128)(2,1)} %get-tuple-element.321, s32[]{:T(128)S(6)} %select_n.88), kind=kOutput, calls=%fused_computation.45.clone.1 | convolution fusion | flops 25165824 | bytes 458820 | tf_op jit(solution)/shard_map/while/body/eval_jaxpr/kbc,kcm->kbm/dot_general | solution.py:76
  438.0 8.7 %fusion.88 = f32[16,16,256]{2,1,0:T(8,128)S(1)} fusion(s32[128,256]{1,0:T(8,128)S(1)} %get-tuple-element.322, s32[16]{0:T(128)S(1)} %add_add_fusion.2, bf16[256,16,128]{2,1,0:T(8,128)(2,1)} %get-tuple-element.321, s32[]{:T(128)S(6)} %select_n.88), kind=kOutput, calls=%fused_computation.45.clone.1 | convolution fusion | flops 25165824 | bytes 458820 | tf_op jit(solution)/shard_map/while/body/eval_jaxpr/kbc,kcm->kbm/dot_general | solution.py:76
  473.1 8.7 %fusion.88 = f32[16,16,256]{2,1,0:T(8,128)S(1)} fusion(s32[128,256]{1,0:T(8,128)S(1)} %get-tuple-element.322, s32[16]{0:T(128)S(1)} %add_add_fusion.2, bf16[256,16,128]{2,1,0:T(8,128)(2,1)} %get-tuple-element.321, s32[]{:T(128)S(6)} %select_n.88), kind=kOutput, calls=%fused_computation.45.clone.1 | convolution fusion | flops 25165824 | bytes 458820 | tf_op jit(solution)/shard_map/while/body/eval_jaxpr/kbc,kcm->kbm/dot_general | solution.py:76
  491.7 8.6 %fusion.90 = f32[16,16,256]{2,1,0:T(8,128)S(1)} fusion(s32[128,256]{1,0:T(8,128)S(1)} %get-tuple-element.322, s32[16]{0:T(128)S(1)} %add_add_fusion.2, bf16[256,16,128]{2,1,0:T(8,128)(2,1)} %get-tuple-element.321, s32[]{:T(128)S(6)} %select_n.88), kind=kOutput, calls=%fused_computation.44.clone.1 | convolution fusion | flops 25165824 | bytes 458820 | tf_op jit(solution)/shard_map/while/body/eval_jaxpr/kbc,kcm->kbm/dot_general | solution.py:72
  508.2 8.7 %fusion.88 = f32[16,16,256]{2,1,0:T(8,128)S(1)} fusion(s32[128,256]{1,0:T(8,128)S(1)} %get-tuple-element.322, s32[16]{0:T(128)S(1)} %add_add_fusion.2, bf16[256,16,128]{2,1,0:T(8,128)(2,1)} %get-tuple-element.321, s32[]{:T(128)S(6)} %select_n.88), kind=kOutput, calls=%fused_computation.45.clone.1 | convolution fusion | flops 25165824 | bytes 458820 | tf_op jit(solution)/shard_map/while/body/eval_jaxpr/kbc,kcm->kbm/dot_general | solution.py:76
  526.9 8.6 %fusion.90 = f32[16,16,256]{2,1,0:T(8,128)S(1)} fusion(s32[128,256]{1,0:T(8,128)S(1)} %get-tuple-element.322, s32[16]{0:T(128)S(1)} %add_add_fusion.2, bf16[256,16,128]{2,1,0:T(8,128)(2,1)} %get-tuple-element.321, s32[]{:T(128)S(6)} %select_n.88), kind=kOutput, calls=%fused_computation.44.clone.1 | convolution fusion | flops 25165824 | bytes 458820 | tf_op jit(solution)/shard_map/while/body/eval_jaxpr/kbc,kcm->kbm/dot_general | solution.py:72
  543.3 8.7 %fusion.88 = f32[16,16,256]{2,1,0:T(8,128)S(1)} fusion(s32[128,256]{1,0:T(8,128)S(1)} %get-tuple-element.322, s32[16]{0:T(128)S(1)} %add_add_fusion.2, bf16[256,16,128]{2,1,0:T(8,128)(2,1)} %get-tuple-element.321, s32[]{:T(128)S(6)} %select_n.88), kind=kOutput, calls=%fused_computation.45.clone.1 | convolution fusion | flops 25165824 | bytes 458820 | tf_op jit(solution)/shard_map/while/body/eval_jaxpr/kbc,kcm->kbm/dot_general | solution.py:76
  578.4 8.7 %fusion.88 = f32[16,16,256]{2,1,0:T(8,128)S(1)} fusion(s32[128,256]{1,0:T(8,128)S(1)} %get-tuple-element.322, s32[16]{0:T(128)S(1)} %add_add_fusion.2, bf16[256,16,128]{2,1,0:T(8,128)(2,1)} %get-tuple-element.321, s32[]{:T(128)S(6)} %select_n.88), kind=kOutput, calls=%fused_computation.45.clone.1 | convolution fusion | flops 25165824 | bytes 458820 | tf_op jit(solution)/shard_map/while/body/eval_jaxpr/kbc,kcm->kbm/dot_general | solution.py:76
  613.5 8.7 %fusion.88 = f32[16,16,256]{2,1,0:T(8,128)S(1)} fusion(s32[128,256]{1,0:T(8,128)S(1)} %get-tuple-element.322, s32[16]{0:T(128)S(1)} %add_add_fusion.2, bf16[256,16,128]{2,1,0:T(8,128)(2,1)} %get-tuple-element.321, s32[]{:T(128)S(6)} %select_n.88), kind=kOutput, calls=%fused_computation.45.clone.1 | convolution fusion | flops 25165824 | bytes 458820 | tf_op jit(solution)/shard_map/while/body/eval_jaxpr/kbc,kcm->kbm/dot_general | solution.py:76
  648.7 8.7 %fusion.88 = f32[16,16,256]{2,1,0:T(8,128)S(1)} fusion(s32[128,256]{1,0:T(8,128)S(1)} %get-tuple-element.322, s32[16]{0:T(128)S(1)} %add_add_fusion.2, bf16[256,16,128]{2,1,0:T(8,128)(2,1)} %get-tuple-element.321, s32[]{:T(128)S(6)} %select_n.88), kind=kOutput, calls=%fused_computation.45.clone.1 | convolution fusion | flops 25165824 | bytes 458820 | tf_op jit(solution)/shard_map/while/body/eval_jaxpr/kbc,kcm->kbm/dot_general | solution.py:76
  683.7 8.7 %fusion.88 = f32[16,16,256]{2,1,0:T(8,128)S(1)} fusion(s32[128,256]{1,0:T(8,128)S(1)} %get-tuple-element.322, s32[16]{0:T(128)S(1)} %add_add_fusion.2, bf16[256,16,128]{2,1,0:T(8,128)(2,1)} %get-tuple-element.321, s32[]{:T(128)S(6)} %select_n.88), kind=kOutput, calls=%fused_computation.45.clone.1 | convolution fusion | flops 25165824 | bytes 458820 | tf_op jit(solution)/shard_map/while/body/eval_jaxpr/kbc,kcm->kbm/dot_general | solution.py:76
  701.1 10.5 %copy.142 = f32[256,2,16,256]{0,2,1,3:T(8,128)} copy(f32[256,2,16,256]{3,2,1,0:T(8,128)} %bitcast.47) | data formatting | bytes 16777216 | tf_op jit(solution)/shard_map/reshape | solution.py:83
  711.6 78.6 %reduce-scatter.2.cloned.1.call-done = f32[256,2,16,64]{0,2,1,3:T(8,128)} async-done(((f32[256,2,16,256]{0,2,1,3:T(8,128)}), f32[256,2,16,64]{0,2,1,3:T(8,128)}) %reduce-scatter.2.cloned.1.call-update) | async-done | bytes 2097168 | tf_op jit(solution)/shard_map/reduce_scatter | solution.py:119
  (165 shorter events, 400.0 us)
Async XLA Ops:
  66.0 11.4 %copy-start = (s32[256,512]{1,0:T(8,128)S(1)}, s32[256,512]{1,0:T(8,128)}, u32[]{:S(2)}) copy-start(s32[256,512]{1,0:T(8,128)} %param.9) | copy-start | bytes 1572868
  66.0 39.6 %all-to-all-start = ((bf16[32,4,1,16,512]{4,3,1,2,0:T(8,128)(2,1)}), bf16[32,4,1,16,512]{4,3,1,2,0:T(8,128)(2,1)S(1)}, u32[]{:S(2)}, u32[]{:S(2)}) async-start(bf16[32,4,1,16,512]{4,3,1,2,0:T(8,128)(2,1)} %constant_dynamic-update-slice_fusion.1), calls=%async_computation | async-start | bytes 4194304 | tf_op jit(solution)/shard_map/all_to_all | solution.py:109
  77.3 712.9 %reduce-scatter.2.cloned.1.call-start = ((), (), s32[]{:S(2)}) async-start(), calls=%async_computation.2 | async-start | bytes 10485760 | tf_op jit(solution)/shard_map/reduce_scatter | solution.py:119
Sparse Core Ops, SparseCore 0:
  711.8 78.4 reduce-scatter.1
